TPU v7x, 256 devices: a whole 4x4x8 slice. The times are simulated.
256 devices in a mesh: dp: 8 (over y_hi, x), ctx: 32 (over y_lo, z, core).
Axes of the slice: x: 4, y: 4 (y_hi: 2, y_lo: 2; y = y_hi * 2 + y_lo), z: 8, core: 2. Of those that a mesh axis runs over, the one named last changes fastest.
Arguments:
- mixed: bfloat16 [8192, 4096], P('ctx', 'dp'), may hold values from -6 to 6
- log_decay: float32 [8192, 16], P('ctx', 'dp'), may hold values from -1 to 0
- beta_logit: float32 [8192, 16], P('ctx', 'dp'), may hold values from -4 to 4
- conv_weight: float32 [4, 4096], P(None, 'dp'), may hold values from -3 to 3
- norm_gain: float32 [128], replicated, may hold values from 0.1 to 1.9
- out_weight: bfloat16 [2048, 1024], P('dp'), may hold values from -0.125 to 0.125
- out_grad: bfloat16 [8192, 1024], P(('ctx', 'dp')), may hold values from -12 to 12
Outputs:
- output: bfloat16 [8192, 1024], P(('ctx', 'dp'))
- grad_mixed: bfloat16 [8192, 4096], P('ctx', 'dp')
- grad_log_decay: float32 [8192, 16], P('ctx', 'dp')
- grad_beta_logit: float32 [8192, 16], P('ctx', 'dp')
- grad_conv_weight: float32 [4, 4096], P(None, 'dp')
- grad_norm_gain: float32 [128], replicated
- grad_out_weight: float32 [2048, 1024], P(('dp', 'ctx'))
All inputs are finite; a program needn't handle non-finite values.
Results may differ from a plain program's by a relative error of at most 0.03.
Values may be sent and summed in bfloat16 or wider, within the bound.
No kernel may reach another device: no remote copies, remote signals or barrier semaphores. Data moves between devices by JAX's collectives and lax.ppermute only.
A program may use at most 128 MiB of HBM per device.

v0:
```python
import math
import jax
import jax.numpy as jnp
from jax import lax
from jax.sharding import PartitionSpec as P

VHEADS = 16
KHEADS = 8
HEADDIM = 128
BLOCK = 64
EPS = 1e-06
HIGHEST = lax.Precision.HIGHEST


def shifted(block, axis, distance):
    devices = range(lax.axis_size(axis))
    route = [(i - distance, i) for i in devices if i - distance in devices]
    return lax.ppermute(block, axis, route)


def prefix_2(value, axis, join, neutral, backward):
    count, mine = (lax.axis_size(axis), lax.axis_index(axis))
    pieces = jax.tree.map(lambda part: lax.all_gather(part, axis), value)
    if backward:
        pieces = jax.tree.map(lambda part: part[::-1], pieces)
        mine = count - 1 - mine
    total = jax.tree.map(
        lambda part, zero: jnp.full_like(part, 0) + jnp.asarray(zero, part.dtype), value, neutral
    )

    def step(position, total):
        longer = join(total, jax.tree.map(lambda part: part[position], pieces))
        return jax.tree.map(lambda new, old: jnp.where(position < mine, new, old), longer, total)

    return lax.fori_loop(0, count - 1, step, total)


def product(pattern, left_array, right_array):
    return jnp.einsum(pattern, left_array, right_array, precision=HIGHEST)


def conv_silu(padded_rows, conv_weight):
    conv_taps = conv_weight.shape[0]
    row_count = padded_rows.shape[0] - (conv_taps - 1)
    summed = jnp.zeros((row_count, padded_rows.shape[1]), jnp.float32)
    for offset in range(conv_taps):
        summed = summed + conv_weight[offset] * padded_rows[offset : offset + row_count]
    return jax.nn.silu(summed)


def unit_rows(vectors):
    return vectors * lax.rsqrt(jnp.sum(vectors * vectors, axis=-1, keepdims=True) + EPS)


def prepare(active, decays, strengths):
    row_count = active.shape[0]
    value_heads = decays.shape[1]
    group_size = VHEADS // KHEADS
    key_heads = value_heads // group_size
    grouped = active.reshape(row_count, key_heads, (2 + group_size) * HEADDIM)
    queries = unit_rows(grouped[:, :, :HEADDIM]) * (1.0 / math.sqrt(HEADDIM))
    key_rows = unit_rows(grouped[:, :, HEADDIM : 2 * HEADDIM])
    values = grouped[:, :, 2 * HEADDIM :].reshape(row_count, value_heads, HEADDIM)
    queries = jnp.repeat(queries, group_size, axis=1)
    key_rows = jnp.repeat(key_rows, group_size, axis=1)
    blocks = row_count // BLOCK

    def arrange(tensor):
        return jnp.transpose(tensor.reshape(blocks, BLOCK, value_heads, -1), (0, 2, 1, 3))

    return (
        arrange(queries),
        arrange(key_rows),
        arrange(values),
        arrange(decays[:, :, None])[..., 0],
        arrange(jax.nn.sigmoid(strengths)[:, :, None])[..., 0],
    )


def block_terms(block_in):
    queries, key_rows, values, decays, strengths = (
        block_in[0],
        block_in[1],
        block_in[2],
        block_in[3],
        block_in[4],
    )
    length = decays.shape[-1]
    cumulative = jnp.cumsum(decays, axis=-1)
    row_index = lax.broadcasted_iota(jnp.int32, (length, length), 0)
    col_index = lax.broadcasted_iota(jnp.int32, (length, length), 1)
    causal = row_index >= col_index
    strict = row_index > col_index
    spread = cumulative[:, :, None] - cumulative[:, None, :]
    damping = jnp.where(causal, jnp.exp(jnp.where(causal, spread, 0.0)), 0.0)
    key_inner = product("hck,hsk->hcs", key_rows, key_rows)
    lower_mat = jnp.where(strict, strengths[:, :, None] * damping * key_inner, 0.0)
    growth = jnp.exp(cumulative)
    tail_keys = jnp.exp(cumulative[:, -1:] - cumulative)[..., None] * key_rows
    stacked = jnp.concatenate(
        [(strengths * growth)[..., None] * key_rows, strengths[..., None] * values], axis=-1
    )
    solved = lax.linalg.triangular_solve(
        lower_mat, stacked, left_side=True, lower=True, unit_diagonal=True
    )
    head_size = key_rows.shape[-1]
    write_keys = solved[..., :head_size]
    new_values = solved[..., head_size:]
    scores = damping * product("hck,hsk->hcs", queries, key_rows)
    return (write_keys, new_values, scores, growth, tail_keys, queries, growth[:, -1])


def rows_layout(stacked):
    return jnp.transpose(stacked, (0, 2, 1, 3)).reshape(
        stacked.shape[0] * stacked.shape[2], stacked.shape[1], stacked.shape[3]
    )


def run_blocks(carry_state, arranged):

    def run_advance(running, block_in):
        write_keys, new_values, scores, growth, tail_keys, queries, growth_end = block_terms(
            block_in
        )
        deltas = new_values - product("hck,hek->hce", write_keys, running)
        output = growth[..., None] * product("hck,hek->hce", queries, running) + product(
            "hcs,hse->hce", scores, deltas
        )
        next_state = growth_end[:, None, None] * running + product(
            "hse,hsk->hek", deltas, tail_keys
        )
        return (next_state, output)

    final_state, outputs = lax.scan(run_advance, carry_state, arranged)
    return (rows_layout(outputs), final_state)


def local_core(carry_state, active, decays, strengths):
    return run_blocks(carry_state, prepare(active, decays, strengths))


def eye_stack(value_heads):
    return jnp.broadcast_to(jnp.eye(HEADDIM, dtype=jnp.float32), (value_heads, HEADDIM, HEADDIM))


def local_pieces(active, decays, strengths):
    identity = eye_stack(decays.shape[1])
    start_carry = (identity, jnp.zeros((decays.shape[1], HEADDIM, HEADDIM), jnp.float32))

    def local_advance(running, block_in):
        through, offset_state = running
        write_keys, new_values, scores, growth, tail_keys, queries, growth_end = block_terms(
            block_in
        )
        effective = growth[..., None] * queries - product("hcs,hsk->hck", scores, write_keys)
        local_out = product("hck,hek->hce", effective, offset_state) + product(
            "hcs,hse->hce", scores, new_values
        )
        reach_rows = product("hck,hjk->hcj", effective, through)
        block_map = growth_end[:, None, None] * identity - product(
            "hsk,hsj->hkj", write_keys, tail_keys
        )
        block_add = product("hse,hsk->hek", new_values, tail_keys)
        through = product("hjk,hkl->hjl", through, block_map)
        offset_state = product("hek,hkl->hel", offset_state, block_map) + block_add
        return ((through, offset_state), (local_out, reach_rows))

    final_pair, outputs = lax.scan(local_advance, start_carry, prepare(active, decays, strengths))
    return (rows_layout(outputs[0]), rows_layout(outputs[1]), final_pair[0], final_pair[1])


def normalize(mixer_out, gain_vector):
    scaled = (
        mixer_out
        * lax.rsqrt(jnp.mean(mixer_out * mixer_out, axis=-1, keepdims=True) + EPS)
        * gain_vector
    )
    return scaled.reshape(mixer_out.shape[0], -1)


def chain_step(earlier_pair, later_pair):
    return (
        product("hjk,hkl->hjl", earlier_pair[0], later_pair[0]),
        product("hek,hkl->hel", earlier_pair[1], later_pair[0]) + later_pair[1],
    )


def local(mixed, log_decay, beta_logit, conv_weight, norm_gain, out_weight, out_grad):
    conv_taps = conv_weight.shape[0]
    row_count = mixed.shape[0]
    value_heads = log_decay.shape[1]
    rim_rows = shifted(mixed[row_count - (conv_taps - 1) :], "ctx", 1)
    padded = jnp.concatenate([rim_rows, mixed], axis=0).astype(jnp.float32)
    active_wide, conv_pull = jax.vjp(conv_silu, padded, conv_weight)
    active = lax.optimization_barrier(active_wide.astype(jnp.bfloat16)).astype(jnp.float32)
    start_pair = (eye_stack(value_heads), jnp.zeros((value_heads, HEADDIM, HEADDIM), jnp.float32))
    pieces_out = local_pieces(active, log_decay, beta_logit)
    chain_maps, chain_adds = (pieces_out[2], pieces_out[3])
    prefix = prefix_2((chain_maps, chain_adds), "ctx", chain_step, start_pair, False)
    entry_state = prefix[1]
    core_out, core_pull = jax.vjp(local_core, entry_state, active, log_decay, beta_logit)
    mixer_out, leaving = core_out
    normed_wide, norm_pull = jax.vjp(normalize, mixer_out, norm_gain)
    normed = normed_wide.astype(jnp.bfloat16)
    result = lax.psum_scatter(
        jnp.dot(normed, out_weight, preferred_element_type=jnp.float32).astype(jnp.bfloat16),
        "dp",
        scatter_dimension=0,
        tiled=True,
    )
    full_grad = lax.all_gather(out_grad, "dp", axis=0, tiled=True)
    back_rows = jnp.dot(full_grad, out_weight.T, preferred_element_type=jnp.float32)
    grad_weight = lax.psum_scatter(
        jnp.einsum("tv,td->vd", normed, full_grad, preferred_element_type=jnp.float32).astype(
            jnp.bfloat16
        ),
        "ctx",
        scatter_dimension=0,
        tiled=True,
    ).astype(jnp.float32)
    grad_mixer, grad_gain = norm_pull(back_rows)
    local_grad = core_pull((grad_mixer, jnp.zeros_like(leaving)))[0]
    suffix = prefix_2(
        (jnp.swapaxes(chain_maps, 1, 2), local_grad), "ctx", chain_step, start_pair, True
    )
    exit_grad = suffix[1]
    core_grads = core_pull((grad_mixer, exit_grad))
    grad_active, grad_decay, grad_beta = (core_grads[1], core_grads[2], core_grads[3])
    grad_padded, grad_conv = conv_pull(grad_active)
    spill_rows = shifted(grad_padded[: conv_taps - 1], "ctx", -1)
    own_rows = grad_padded[conv_taps - 1 :]
    own_rows = own_rows.at[row_count - (conv_taps - 1) :].add(spill_rows)
    grad_conv_total, gain_partial = lax.psum((grad_conv, grad_gain), "ctx")
    grad_gain_total = lax.psum(gain_partial, "dp")
    return (
        result,
        own_rows.astype(jnp.bfloat16),
        grad_decay,
        grad_beta,
        grad_conv_total,
        grad_gain_total,
        grad_weight,
    )


def solution(mesh):
    return jax.shard_map(
        local,
        mesh=mesh,
        in_specs=(
            P("ctx", "dp"),
            P("ctx", "dp"),
            P("ctx", "dp"),
            P(None, "dp"),
            P(),
            P("dp", None),
            P(("ctx", "dp"), None),
        ),
        out_specs=(
            P(("ctx", "dp"), None),
            P("ctx", "dp"),
            P("ctx", "dp"),
            P("ctx", "dp"),
            P(None, "dp"),
            P(),
            P(("dp", "ctx"), None),
        ),
        check_vma=False,
    )
```

profile of v0, /device:TPU:8, one launch (start us, length us, event | category | flops | bytes accessed | tf_op | source)
XLA Modules:
  0.0 858.3 jit_solution(8584469403035977819)
XLA Ops:
  8.0 1.9 collective-permute-start
  12.5 3.9 collective-permute-done
  20.2 52.3 %while.145 = (s32[]{:T(128)}, f32[2,128,128]{1,2,0:T(8,128)S(1)}, f32[2,128,128]{1,2,0:T(8,128)S(1)}, f32[4,2,64]{2,1,0:T(2,128)S(1)}, f32[4,2,64]{2,1,0:T(2,128...) while((s32[]{:T(128)}, f32[2,128,128]{1,2,0:T(8,128)S(1)}, ...), condition=%wide.region_3.5_spmd.clone, body=%wide.region_1.4_spmd.clone.sunk | while | flops 189067456 | bytes 2523331 | solution.py:168
  21.2 9.8 %custom-call.44 = f32[2,1,64,64]{2,3,1,0:T(8,128)S(1)} custom-call(f32[2,1,64,64]{3,2,1,0:T(8,128)S(1)} %fusion.384), custom_call_target="InvertDiagBlocksLowerTriangular" | custom-call | tf_op jit(solution)/shard_map/while/body/eval_jaxpr/triangular_solve/custom-call.1 | solution.py:103
  34.3 9.8 %custom-call.44 = f32[2,1,64,64]{2,3,1,0:T(8,128)S(1)} custom-call(f32[2,1,64,64]{3,2,1,0:T(8,128)S(1)} %fusion.384), custom_call_target="InvertDiagBlocksLowerTriangular" | custom-call | tf_op jit(solution)/shard_map/while/body/eval_jaxpr/triangular_solve/custom-call.1 | solution.py:103
  47.3 9.8 %custom-call.44 = f32[2,1,64,64]{2,3,1,0:T(8,128)S(1)} custom-call(f32[2,1,64,64]{3,2,1,0:T(8,128)S(1)} %fusion.384), custom_call_target="InvertDiagBlocksLowerTriangular" | custom-call | tf_op jit(solution)/shard_map/while/body/eval_jaxpr/triangular_solve/custom-call.1 | solution.py:103
  60.4 9.8 %custom-call.44 = f32[2,1,64,64]{2,3,1,0:T(8,128)S(1)} custom-call(f32[2,1,64,64]{3,2,1,0:T(8,128)S(1)} %fusion.384), custom_call_target="InvertDiagBlocksLowerTriangular" | custom-call | tf_op jit(solution)/shard_map/while/body/eval_jaxpr/triangular_solve/custom-call.1 | solution.py:103
  74.3 35.2 %all_gather.33 = bf16[256,1024]{1,0:T(8,128)(2,1)S(1)} all-gather(bf16[32,1024]{1,0:T(8,128)(2,1)S(1)} %copy-done.9), channel_id=1, replica_groups=mesh['dp'=8,'ctx'=32] {'dp'}, dimensions={0}, use_global_device_ids=true | all-gather | bytes 589824 | tf_op jit(solution)/shard_map/all_gather | solution.py:211
  111.7 28.6 %all-gather.9.cloned.1.call-done = f32[64,128,128]{2,1,0:T(8,128)} async-done(((f32[2,128,128]{2,1,0:T(8,128)}), f32[64,128,128]{2,1,0:T(8,128)}) %all-gather.9.cloned.1.call-update) | async-done | bytes 4194320 | tf_op jit(solution)/shard_map/all_gather | solution.py:23
  140.3 68.5 %all-gather.11.cloned.1.call-done = f32[64,128,128]{2,1,0:T(8,128)} async-done(((f32[2,128,128]{2,1,0:T(8,128)}), f32[64,128,128]{2,1,0:T(8,128)}) %all-gather.11.cloned.1.call-update) | async-done | bytes 4194320 | tf_op jit(solution)/shard_map/all_gather | solution.py:23
  208.8 73.6 %while.146 = (s32[]{:T(128)}, f32[2,128,128]{1,2,0:T(8,128)S(1)}, s32[]{:T(128)}, f32[32,2,128,128]{3,2,1,0:T(8,128)}, f32[32,2,128,128]{3,2,1,0:T(8,128)}, /*index=5*/s32[]{:T(128)}, s32[]{:T(128)}) while((s32[]{:T(128)}, f32[2,128,128]{1,2,0:T(8,128)S(1)}, s32[]{:T(128)}, f32[32,2,128,128]{3,2,1,0:T(8,128)}, ...), condition=%wide.region_5.7_spmd.clone, body=%wide.region_4.6_spmd.clone.sunk | while | flops 50462724 | bytes 1443947 | solution.py:35
  209.9 1.3 fusion.388
  212.3 1.3 fusion.388
  226.5 1.3 fusion.388
  233.6 1.3 fusion.388
  238.4 1.3 fusion.388
  240.7 1.3 fusion.388
  245.5 1.3 fusion.388
  257.3 1.3 fusion.388
  262.1 1.3 fusion.388
  264.5 1.3 fusion.388
  266.8 1.3 fusion.388
  287.1 97.9 %while.143 = (s32[]{:T(128)}, f32[2,128,128]{2,1,0:T(8,128)S(1)}, f32[4,2,64,128]{3,2,1,0:T(8,128)}, f32[4,2,64,64]{3,2,1,0:T(8,128)}, f32[4,2,64,64]{3,2,1,0:T(...) while((s32[]{:T(128)}, f32[2,128,128]{2,1,0:T(8,128)S(1)}, ...), condition=%wide.region_9.11_spmd.clone.clone, body=%wide.region_7.10_spmd.clone.clone.sunk | while | flops 138834496 | bytes 3687305 | solution.py:134
  292.7 11.2 %custom-call.42 = f32[2,1,64,64]{2,3,1,0:T(8,128)} custom-call(f32[2,1,64,64]{3,2,1,0:T(8,128)} %get-tuple-element.3230), custom_call_target="InvertDiagBlocksLowerTriangular" | custom-call | tf_op jit(solution)/shard_map/jvp()/while/body/eval_jaxpr/triangular_solve/custom-call.1 | solution.py:103
  303.9 1.8 bitcast_dynamic-update-slice_fusion.19
  308.2 1.3 constant_dynamic-update-slice_fusion.15
  317.2 11.2 %custom-call.42 = f32[2,1,64,64]{2,3,1,0:T(8,128)} custom-call(f32[2,1,64,64]{3,2,1,0:T(8,128)} %get-tuple-element.3230), custom_call_target="InvertDiagBlocksLowerTriangular" | custom-call | tf_op jit(solution)/shard_map/jvp()/while/body/eval_jaxpr/triangular_solve/custom-call.1 | solution.py:103
  328.4 1.8 bitcast_dynamic-update-slice_fusion.19
  341.6 11.2 %custom-call.42 = f32[2,1,64,64]{2,3,1,0:T(8,128)} custom-call(f32[2,1,64,64]{3,2,1,0:T(8,128)} %get-tuple-element.3230), custom_call_target="InvertDiagBlocksLowerTriangular" | custom-call | tf_op jit(solution)/shard_map/jvp()/while/body/eval_jaxpr/triangular_solve/custom-call.1 | solution.py:103
  352.8 1.8 bitcast_dynamic-update-slice_fusion.19
  366.1 11.2 %custom-call.42 = f32[2,1,64,64]{2,3,1,0:T(8,128)} custom-call(f32[2,1,64,64]{3,2,1,0:T(8,128)} %get-tuple-element.3230), custom_call_target="InvertDiagBlocksLowerTriangular" | custom-call | tf_op jit(solution)/shard_map/jvp()/while/body/eval_jaxpr/triangular_solve/custom-call.1 | solution.py:103
  377.3 1.8 bitcast_dynamic-update-slice_fusion.19
  381.6 1.3 constant_dynamic-update-slice_fusion.15
  390.1 2.2 convolution_convert_fusion
  392.4 18.6 %while.147 = (s32[]{:T(128)}, f32[2,128,128]{2,1,0:T(8,128)S(1)}, f32[4,2,1,1]{1,3,2,0:T(1,128)}, f32[4,2,64,1]{2,1,3,0:T(2,128)S(1)}, f32[4,2,64,128]{3,2,1,0:T...) while((s32[]{:T(128)}, f32[2,128,128]{2,1,0:T(8,128)S(1)}, ...), condition=%wide.region_14.16_spmd.clone, body=%wide.region_13.15_spmd.clone.sunk | while | flops 88293376 | bytes 1316019 | solution.py:134
  412.0 5.6 copy.142
  417.7 4.7 rev.6
  424.0 83.7 %reduce-scatter.5.cloned.1.call-done = bf16[8,1024]{1,0:T(8,128)(2,1)} async-done(((bf16[256,1024]{1,0:T(8,128)(2,1)}), bf16[8,1024]{1,0:T(8,128)(2,1)}) %reduce-scatter.5.cloned.1.call-update) | async-done | bytes 16400 | tf_op jit(solution)/shard_map/reduce_scatter | solution.py:213
  507.7 1.3 convert_element_type.34
  509.0 63.3 %all-gather.15.cloned.1.call-done = f32[64,128,128]{2,1,0:T(8,128)} async-done(((f32[2,128,128]{2,1,0:T(8,128)}), f32[64,128,128]{2,1,0:T(8,128)}) %all-gather.15.cloned.1.call-update) | async-done | bytes 4194320 | tf_op jit(solution)/shard_map/all_gather | solution.py:23
  572.4 5.6 copy.145
  578.0 4.7 rev.7
  582.6 40.0 %while.148 = (s32[]{:T(128)}, f32[2,128,128]{1,2,0:T(8,128)S(1)}, s32[]{:T(128)}, f32[32,2,128,128]{2,3,1,0:T(8,128)}, f32[32,2,128,128]{2,3,1,0:T(8,128)}, /*index=5*/s32[]{:T(128)}, s32[]{:T(128)}) while((s32[]{:T(128)}, f32[2,128,128]{1,2,0:T(8,128)S(1)}, s32[]{:T(128)}, f32[32,2,128,128]{2,3,1,0:T(8,128)}, ...), condition=%wide.region_16.18_spmd.clone, body=%wide.region_15.17_spmd.clone.sunk | while | flops 50462724 | bytes 920167 | solution.py:35
  624.9 133.3 %while.144 = (s32[]{:T(128)}, f32[2,128,128]{2,1,0:T(8,128)S(1)}, f32[4,2,64,128]{3,2,1,0:T(8,128)}, f32[4,2,64,128]{3,2,1,0:T(8,128)}, f32[4,2,64,128]{3,2,1,0:...) while((s32[]{:T(128)}, f32[2,128,128]{2,1,0:T(8,128)S(1)}, ...), condition=%wide.region_28.30_spmd.clone.clone, body=%wide.region_17.29_spmd.clone.clone.sunk | while | flops 283874368 | bytes 5498349 | solution.py:134
  627.6 1.5 add_bitcast_fusion.3
  629.1 10.6 %custom-call.43 = f32[2,1,64,64]{2,3,1,0:T(8,128)S(1)} custom-call(f32[2,1,64,64]{3,2,1,0:T(8,128)} %add_bitcast_fusion.3), custom_call_target="InvertDiagBlocksLowerTriangular" | custom-call | tf_op jit(solution)/shard_map/transpose(jvp())/while/body/eval_jaxpr/triangular_solve | solution.py:103
  645.5 1.7 fusion.359
  653.3 1.7 fusion.369
  660.9 1.5 add_bitcast_fusion.3
  662.4 10.6 %custom-call.43 = f32[2,1,64,64]{2,3,1,0:T(8,128)S(1)} custom-call(f32[2,1,64,64]{3,2,1,0:T(8,128)} %add_bitcast_fusion.3), custom_call_target="InvertDiagBlocksLowerTriangular" | custom-call | tf_op jit(solution)/shard_map/transpose(jvp())/while/body/eval_jaxpr/triangular_solve | solution.py:103
  678.9 1.7 fusion.359
  686.6 1.7 fusion.369
  694.3 1.5 add_bitcast_fusion.3
  695.7 10.6 %custom-call.43 = f32[2,1,64,64]{2,3,1,0:T(8,128)S(1)} custom-call(f32[2,1,64,64]{3,2,1,0:T(8,128)} %add_bitcast_fusion.3), custom_call_target="InvertDiagBlocksLowerTriangular" | custom-call | tf_op jit(solution)/shard_map/transpose(jvp())/while/body/eval_jaxpr/triangular_solve | solution.py:103
  712.1 1.7 fusion.359
  719.9 1.7 fusion.369
  727.5 1.5 add_bitcast_fusion.3
  729.0 10.6 %custom-call.43 = f32[2,1,64,64]{2,3,1,0:T(8,128)S(1)} custom-call(f32[2,1,64,64]{3,2,1,0:T(8,128)} %add_bitcast_fusion.3), custom_call_target="InvertDiagBlocksLowerTriangular" | custom-call | tf_op jit(solution)/shard_map/transpose(jvp())/while/body/eval_jaxpr/triangular_solve | solution.py:103
  745.5 1.7 fusion.359
  753.2 1.7 fusion.369
  763.2 1.5 multiply_reduce_fusion.3
  765.4 4.1 collective-permute-start.1
  770.9 55.8 %all-reduce.15 = (f32[4,512]{1,0:T(4,128)}, f32[128]{0:T(128)S(1)}) all-reduce(f32[4,512]{1,0:T(4,128)S(1)} %pad_add_fusion.5, f32[128]{0:T(128)S(1)} %copy-done.26), channel_id=1, replica_groups=mesh['dp'=8,'ctx'=32] {'ctx'}, use_global_device_ids=true, to_apply=%region_37.39 | all-reduce | flops 2176 | bytes 17408 | tf_op jit(solution)/shard_map/psum | solution.py:233
  826.7 23.8 %psum.23 = f32[128]{0:T(128)} all-reduce(f32[128]{0:T(128)S(1)} %get-tuple-element.2610), channel_id=1, replica_groups=mesh['dp'=8,'ctx'=32] {'dp'}, use_global_device_ids=true, to_apply=%region_41.43 | all-reduce | flops 128 | bytes 1024 | tf_op jit(solution)/shard_map/psum | solution.py:234
  (637 shorter events, 275.1 us)
Async XLA Ops:
  7.2 103.3 %copy-start = (bf16[256,1024]{1,0:T(8,128)(2,1)S(1)}, bf16[256,1024]{1,0:T(8,128)(2,1)}, u32[]{:S(2)}) copy-start(bf16[256,1024]{1,0:T(8,128)(2,1)} %param.28) | copy-start | bytes 1572868
  7.2 133.1 %all-gather.9.cloned.1.call-start = ((), (), s32[]{:S(2)}) async-start(), calls=%async_computation.4 | async-start | bytes 4325376 | tf_op jit(solution)/shard_map/all_gather | solution.py:23
  8.0 8.4 collective-permute-start
  11.5 7.5 copy-start.14
  11.5 7.5 copy-start.16
  11.5 7.5 copy-start.18
  11.5 8.7 %copy-start.12 = (f32[1,512]{1,0:T(1,128)}, f32[1,512]{1,0:T(1,128)S(1)}, u32[]{:S(2)}) copy-start(f32[1,512]{1,0:T(1,128)S(1)} %get-tuple-element.2670) | copy-start | bytes 6148
  18.7 0.6 copy-start.21
  18.7 0.6 copy-start.22
  18.8 1.3 copy-start.20
  20.1 54.2 %copy-start.9 = (bf16[32,1024]{1,0:T(8,128)(2,1)S(1)}, bf16[32,1024]{1,0:T(8,128)(2,1)}, u32[]{:S(2)}) copy-start(bf16[32,1024]{1,0:T(8,128)(2,1)} %param.29) | copy-start | bytes 196612
  20.2 91.5 %copy-start.24 = (f32[128]{0:T(128)S(1)}, f32[128]{0:T(128)}, u32[]{:S(2)}) copy-start(f32[128]{0:T(128)} %param.27) | copy-start | bytes 1540
  72.5 39.2 %copy-start.2 = (f32[2,128,128]{1,2,0:T(8,128)}, f32[2,128,128]{1,2,0:T(8,128)S(1)}, u32[]{:S(2)}) copy-start(f32[2,128,128]{1,2,0:T(8,128)S(1)} %get-tuple-element.1689) | copy-start | bytes 393220
  72.5 136.3 %copy-start.8 = (f32[4,2,64]{2,1,0:T(2,128)}, f32[4,2,64]{2,1,0:T(2,128)S(1)}, u32[]{:S(2)}) copy-start(f32[4,2,64]{2,1,0:T(2,128)S(1)} %get-tuple-element.3692) | copy-start | bytes 6148
  72.5 136.3 %copy-start.10 = (f32[4,2,64]{2,1,0:T(2,128)}, f32[4,2,64]{2,1,0:T(2,128)S(1)}, u32[]{:S(2)}) copy-start(f32[4,2,64]{2,1,0:T(2,128)S(1)} %get-tuple-element.3696) | copy-start | bytes 6148
  73.3 135.5 %all-gather.11.cloned.1.call-start = ((), (), s32[]{:S(2)}) async-start(), calls=%async_computation.5 | async-start | bytes 4325376 | tf_op jit(solution)/shard_map/all_gather | solution.py:23
  74.1 337.9 %all-gather.13.cloned.1.call-start = ((), (), s32[]{:S(2)}) async-start(), calls=%async_computation.6 | async-start | bytes 4325376 | tf_op jit(solution)/shard_map/all_gather | solution.py:23
  109.6 0.8 copy-start.3
  110.8 0.8 copy-start.4
  111.7 396.0 %reduce-scatter.5.cloned.1.call-start = ((), (), s32[]{:S(2)}) async-start(), calls=%async_computation.3 | async-start | bytes 540672 | tf_op jit(solution)/shard_map/reduce_scatter | solution.py:213
  208.8 78.2 %copy-start.11 = (f32[4,2,64,1]{2,1,3,0:T(2,128)S(1)}, f32[4,2,64,1]{2,1,3,0:T(2,128)}, u32[]{:S(2)}) copy-start(f32[4,2,64,1]{2,1,3,0:T(2,128)} %custom-call.36) | copy-start | bytes 6148
  287.1 97.9 %copy-start.25 = (f32[128]{0:T(128)S(1)}, f32[128]{0:T(128)}, u32[]{:S(2)}) copy-start(f32[128]{0:T(128)} %param.27) | copy-start | bytes 1540
  390.1 2.3 copy-start.5
  392.3 180.1 %all-gather.15.cloned.1.call-start = ((), (), s32[]{:S(2)}) async-start(), calls=%async_computation.7 | async-start | bytes 4325376 | tf_op jit(solution)/shard_map/all_gather | solution.py:23
  411.0 0.7 copy-start.1
  411.7 439.1 %reduce-scatter.3.cloned.1.call-start = ((), (), s32[]{:S(2)}) async-start(), calls=%async_computation.2 | async-start | bytes 589824 | tf_op jit(solution)/shard_map/reduce_scatter | solution.py:205
  417.7 5.2 copy-start.6
  758.2 6.6 copy-start.13
  758.2 6.6 copy-start.15
  758.2 6.6 copy-start.17
  758.2 6.6 copy-start.19
  764.7 5.6 copy-start.23
  764.7 6.2 copy-start.26
  765.4 85.1 %collective-permute-start.1 = (f32[3,512]{1,0:T(4,128)S(1)}, f32[3,512]{1,0:T(4,128)S(1)}, u32[]{:S(2)}, u32[]{:S(2)}) collective-permute-start(f32[3,512]{1,0:T(4,128)S(1)} %pad_add_fusion.4), channel_id=1, source_target_pairs={{1,0},{2,1},{3,2},{4,3},{5,4},{6,5},{7,6},{8,7},{9,8},{10,9},{11,1... | collective-permute-start | bytes 18440 | tf_op jit(solution)/shard_map/ppermute | solution.py:18
  850.7 0.7 copy-start.7
Sparse Core Ops, SparseCore 0:
  73.4 66.8 all-gather.8
  142.2 66.6 all-gather.10
  210.7 66.4 all-gather.12
  392.4 115.2 reduce-scatter.4
  509.6 62.7 all-gather.14
  577.2 75.5 reduce-scatter.2
where the time goes:
time: 865 us; the launch traced here: 858 us
  waiting for transfers between devices  248 us (29%)
  matrix products  195 us (23%)
  other arithmetic  179 us (21%)
  blocking collectives  115 us (13%)
  local copies, waits for them, and re-layouts  95.8 us (11%)
  between operations  14.9 us (2%)
    dot_general x170, matrix products, product(): return jnp.einsum(pattern, left_array, right_array, precision=HIGHEST)  172 us
    all_gather x4, waiting for transfers between devices, prefix_2(): pieces = jax.tree.map(lambda part: lax.all_gather(part, axis), value)  160 us
    another operation x48, other arithmetic, block_terms(): lax.linalg.triangular_solve(lower_mat, stacked, left_side=True, lower=Tru...  133 us
    reduce_scatter x1, waiting for transfers between devices, local(): lax.psum_scatter(jnp.einsum('tv,td->vd', normed, full_grad, preferred_ele...  83.7 us
    psum x1, blocking collectives, local(): grad_conv_total, gain_partial = lax.psum((grad_conv, grad_gain), 'ctx')  55.8 us
    all_gather x1, blocking collectives, local(): full_grad = lax.all_gather(out_grad, 'dp', axis=0, tiled=True)  35.2 us
    dynamic_slice x62, local copies, waits for them, and re-layouts, step(): longer = join(total, jax.tree.map(lambda part: part[position], pieces))  31.4 us
    psum x1, blocking collectives, local(): grad_gain_total = lax.psum(gain_partial, 'dp')  23.8 us
  transfers between devices with their start and end apart: 8, of which 5 were waited for; matrix products, arithmetic and copies ran while one was open for 48% of the time, Pallas kernels for 0%

commit v1 on v0

--- a/solution.py
+++ b/solution.py
@@ -10,6 +10,13 @@
 BLOCK = 64
 EPS = 1e-06
 HIGHEST = lax.Precision.HIGHEST
+
+
+def exchange_gather(block, axis, along):
+    count = lax.axis_size(axis)
+    blocks = jnp.stack([block for _ in range(count)])
+    blocks = lax.all_to_all(blocks, axis, split_axis=0, concat_axis=0)
+    return jnp.concatenate(blocks, axis=along)
 
 
 def shifted(block, axis, distance):
@@ -208,7 +215,7 @@
         scatter_dimension=0,
         tiled=True,
     )
-    full_grad = lax.all_gather(out_grad, "dp", axis=0, tiled=True)
+    full_grad = exchange_gather(out_grad, "dp", 0)
     back_rows = jnp.dot(full_grad, out_weight.T, preferred_element_type=jnp.float32)
     grad_weight = lax.psum_scatter(
         jnp.einsum("tv,td->vd", normed, full_grad, preferred_element_type=jnp.float32).astype(

time: 865 us -> 833 us (0.963)
  blocking collectives: 115 us -> 79.6 us
  waiting for transfers between devices: 248 us -> 276 us
  other arithmetic: 179 us -> 156 us
    all_gather x1 -> x0, blocking collectives: 35.2 us -> none  [local(): full_grad = lax.all_gather(out_grad, 'dp', axis=0, tiled=True)]
    all_gather x4, waiting for transfers between devices: 160 us -> 190 us  [prefix_2(): pieces = jax.tree.map(lambda part: lax.all_gather(part, axis), value)]
    another operation x48, other arithmetic: 133 us -> 122 us  [block_terms(): lax.linalg.triangular_solve(lower_mat, stacked, left_side=True, lower=Tru...]
  transfers between devices with their start and end apart: 8 -> 9, of which waited for: 5 -> 5; matrix products, arithmetic and copies ran while one was open for 48% -> 46% of each run, Pallas kernels for 0% -> 0%
where the time goes in v1:
time: 833 us; the launch traced here: 827 us
  waiting for transfers between devices  276 us (33%)
  matrix products  192 us (23%)
  other arithmetic  156 us (19%)
  local copies, waits for them, and re-layouts  91.5 us (11%)
  blocking collectives  79.6 us (10%)
  between operations  14.9 us (2%)
  starting transfers between devices  12.8 us (2%)
    all_gather x4, waiting for transfers between devices, prefix_2(): pieces = jax.tree.map(lambda part: lax.all_gather(part, axis), value)  190 us
    dot_general x170, matrix products, product(): return jnp.einsum(pattern, left_array, right_array, precision=HIGHEST)  169 us
    another operation x48, other arithmetic, block_terms(): lax.linalg.triangular_solve(lower_mat, stacked, left_side=True, lower=Tru...  122 us
    reduce_scatter x1, waiting for transfers between devices, local(): lax.psum_scatter(jnp.einsum('tv,td->vd', normed, full_grad, preferred_ele...  82 us
    psum x1, blocking collectives, local(): grad_conv_total, gain_partial = lax.psum((grad_conv, grad_gain), 'ctx')  55.8 us
    dynamic_slice x62, local copies, waits for them, and re-layouts, step(): longer = join(total, jax.tree.map(lambda part: part[position], pieces))  31.4 us
    psum x1, blocking collectives, local(): grad_gain_total = lax.psum(gain_partial, 'dp')  23.8 us
  transfers between devices with their start and end apart: 9, of which 5 were waited for; matrix products, arithmetic and copies ran while one was open for 46% of the time, Pallas kernels for 0%

profile of v1, /device:TPU:8, one launch (start us, length us, event | category | flops | bytes accessed | tf_op | source)
XLA Modules:
  0.0 827.1 jit_solution(1264442451991390190)
XLA Ops:
  8.0 1.9 collective-permute-start
  12.5 3.9 collective-permute-done
  19.4 52.3 %while.145 = (s32[]{:T(128)}, f32[2,128,128]{1,2,0:T(8,128)S(1)}, f32[2,128,128]{1,2,0:T(8,128)S(1)}, f32[4,2,64]{2,1,0:T(2,128)S(1)}, f32[4,2,64]{2,1,0:T(2,128...) while((s32[]{:T(128)}, f32[2,128,128]{1,2,0:T(8,128)S(1)}, ...), condition=%wide.region_3.5_spmd.clone, body=%wide.region_1.4_spmd.clone.sunk | while | flops 189067456 | bytes 2523323 | solution.py:175
  20.3 9.8 %custom-call.44 = f32[2,1,64,64]{2,3,1,0:T(8,128)S(1)} custom-call(f32[2,1,64,64]{3,2,1,0:T(8,128)S(1)} %fusion.389), custom_call_target="InvertDiagBlocksLowerTriangular" | custom-call | tf_op jit(solution)/shard_map/while/body/eval_jaxpr/triangular_solve/custom-call.1 | solution.py:110
  33.4 9.8 %custom-call.44 = f32[2,1,64,64]{2,3,1,0:T(8,128)S(1)} custom-call(f32[2,1,64,64]{3,2,1,0:T(8,128)S(1)} %fusion.389), custom_call_target="InvertDiagBlocksLowerTriangular" | custom-call | tf_op jit(solution)/shard_map/while/body/eval_jaxpr/triangular_solve/custom-call.1 | solution.py:110
  46.5 9.8 %custom-call.44 = f32[2,1,64,64]{2,3,1,0:T(8,128)S(1)} custom-call(f32[2,1,64,64]{3,2,1,0:T(8,128)S(1)} %fusion.389), custom_call_target="InvertDiagBlocksLowerTriangular" | custom-call | tf_op jit(solution)/shard_map/while/body/eval_jaxpr/triangular_solve/custom-call.1 | solution.py:110
  59.6 9.8 %custom-call.44 = f32[2,1,64,64]{2,3,1,0:T(8,128)S(1)} custom-call(f32[2,1,64,64]{3,2,1,0:T(8,128)S(1)} %fusion.389), custom_call_target="InvertDiagBlocksLowerTriangular" | custom-call | tf_op jit(solution)/shard_map/while/body/eval_jaxpr/triangular_solve/custom-call.1 | solution.py:110
  74.2 6.3 all-to-all-start
  81.3 58.9 %all-gather.9.cloned.1.call-done = f32[64,128,128]{2,1,0:T(8,128)} async-done(((f32[2,128,128]{2,1,0:T(8,128)}), f32[64,128,128]{2,1,0:T(8,128)}) %all-gather.9.cloned.1.call-update) | async-done | bytes 4194320 | tf_op jit(solution)/shard_map/all_gather | solution.py:30
  140.2 67.6 %all-gather.11.cloned.1.call-done = f32[64,128,128]{2,1,0:T(8,128)} async-done(((f32[2,128,128]{2,1,0:T(8,128)}), f32[64,128,128]{2,1,0:T(8,128)}) %all-gather.11.cloned.1.call-update) | async-done | bytes 4194320 | tf_op jit(solution)/shard_map/all_gather | solution.py:30
  207.8 73.6 %while.146 = (s32[]{:T(128)}, f32[2,128,128]{1,2,0:T(8,128)S(1)}, s32[]{:T(128)}, f32[32,2,128,128]{3,2,1,0:T(8,128)}, f32[32,2,128,128]{3,2,1,0:T(8,128)}, /*index=5*/s32[]{:T(128)}, s32[]{:T(128)}) while((s32[]{:T(128)}, f32[2,128,128]{1,2,0:T(8,128)S(1)}, s32[]{:T(128)}, f32[32,2,128,128]{3,2,1,0:T(8,128)}, ...), condition=%wide.region_5.7_spmd.clone, body=%wide.region_4.6_spmd.clone.sunk | while | flops 50462724 | bytes 1443939 | solution.py:42
  211.2 1.3 fusion.393
  216.0 1.3 fusion.393
  220.7 1.3 fusion.393
  223.1 1.3 fusion.393
  225.5 1.3 fusion.393
  227.8 1.3 fusion.393
  230.2 1.3 fusion.393
  232.6 1.3 fusion.393
  237.3 1.3 fusion.393
  239.7 1.3 fusion.393
  244.5 1.3 fusion.393
  246.8 1.3 fusion.393
  251.6 1.3 fusion.393
  256.3 1.3 fusion.393
  258.7 1.3 fusion.393
  261.1 1.3 fusion.393
  263.4 1.3 fusion.393
  265.8 1.3 fusion.393
  275.3 1.3 fusion.393
  284.5 76.2 %while.143 = (s32[]{:T(128)}, f32[2,128,128]{2,1,0:T(8,128)S(1)}, f32[4,2,64,128]{3,2,1,0:T(8,128)S(1)}, f32[4,2,64,64]{3,2,1,0:T(8,128)}, f32[4,2,64,64]{3,2,1,...) while((s32[]{:T(128)}, f32[2,128,128]{2,1,0:T(8,128)S(1)}, ...), condition=%wide.region_9.11_spmd.clone.clone, body=%wide.region_7.10_spmd.clone.clone.sunk | while | flops 138834496 | bytes 3690345 | solution.py:141
  287.0 9.8 %custom-call.42 = f32[2,1,64,64]{2,3,1,0:T(8,128)S(1)} custom-call(f32[2,1,64,64]{3,2,1,0:T(8,128)S(1)} %get-tuple-element.3142), custom_call_target="InvertDiagBlocksLowerTriangular" | custom-call | tf_op jit(solution)/shard_map/jvp()/while/body/eval_jaxpr/triangular_solve/custom-call.1 | solution.py:110
  306.0 9.8 %custom-call.42 = f32[2,1,64,64]{2,3,1,0:T(8,128)S(1)} custom-call(f32[2,1,64,64]{3,2,1,0:T(8,128)S(1)} %get-tuple-element.3142), custom_call_target="InvertDiagBlocksLowerTriangular" | custom-call | tf_op jit(solution)/shard_map/jvp()/while/body/eval_jaxpr/triangular_solve/custom-call.1 | solution.py:110
  325.0 9.8 %custom-call.42 = f32[2,1,64,64]{2,3,1,0:T(8,128)S(1)} custom-call(f32[2,1,64,64]{3,2,1,0:T(8,128)S(1)} %get-tuple-element.3142), custom_call_target="InvertDiagBlocksLowerTriangular" | custom-call | tf_op jit(solution)/shard_map/jvp()/while/body/eval_jaxpr/triangular_solve/custom-call.1 | solution.py:110
  344.1 9.8 %custom-call.42 = f32[2,1,64,64]{2,3,1,0:T(8,128)S(1)} custom-call(f32[2,1,64,64]{3,2,1,0:T(8,128)S(1)} %get-tuple-element.3142), custom_call_target="InvertDiagBlocksLowerTriangular" | custom-call | tf_op jit(solution)/shard_map/jvp()/while/body/eval_jaxpr/triangular_solve/custom-call.1 | solution.py:110
  361.0 2.0 fusion.222
  363.6 2.2 convolution_convert_fusion
  365.8 18.7 %while.147 = (s32[]{:T(128)}, f32[2,128,128]{2,1,0:T(8,128)S(1)}, f32[4,2,1,1]{1,3,2,0:T(1,128)}, f32[4,2,64,1]{2,1,3,0:T(2,128)S(1)}, f32[4,2,64,128]{3,2,1,0:T...) while((s32[]{:T(128)}, f32[2,128,128]{2,1,0:T(8,128)S(1)}, ...), condition=%wide.region_14.16_spmd.clone, body=%wide.region_13.15_spmd.clone.sunk | while | flops 88293376 | bytes 1316011 | solution.py:141
  385.7 5.6 copy.108
  391.4 4.6 rev.6
  396.8 2.0 convolution_convert_fusion.1
  398.9 82.0 %reduce-scatter.5.cloned.1.call-done = bf16[8,1024]{1,0:T(8,128)(2,1)} async-done(((bf16[256,1024]{1,0:T(8,128)(2,1)}), bf16[8,1024]{1,0:T(8,128)(2,1)}) %reduce-scatter.5.cloned.1.call-update) | async-done | bytes 16400 | tf_op jit(solution)/shard_map/reduce_scatter | solution.py:220
  480.9 1.3 convert_element_type.41
  482.2 63.4 %all-gather.15.cloned.1.call-done = f32[64,128,128]{2,1,0:T(8,128)} async-done(((f32[2,128,128]{2,1,0:T(8,128)}), f32[64,128,128]{2,1,0:T(8,128)}) %all-gather.15.cloned.1.call-update) | async-done | bytes 4194320 | tf_op jit(solution)/shard_map/all_gather | solution.py:30
  545.6 5.6 copy.112
  551.2 4.7 rev.7
  555.8 40.0 %while.148 = (s32[]{:T(128)}, f32[2,128,128]{1,2,0:T(8,128)S(1)}, s32[]{:T(128)}, f32[32,2,128,128]{2,3,1,0:T(8,128)}, f32[32,2,128,128]{2,3,1,0:T(8,128)}, /*index=5*/s32[]{:T(128)}, s32[]{:T(128)}) while((s32[]{:T(128)}, f32[2,128,128]{1,2,0:T(8,128)S(1)}, s32[]{:T(128)}, f32[32,2,128,128]{2,3,1,0:T(8,128)}, ...), condition=%wide.region_16.18_spmd.clone, body=%wide.region_15.17_spmd.clone.sunk | while | flops 50462724 | bytes 920159 | solution.py:42
  599.3 127.7 %while.144 = (s32[]{:T(128)}, f32[2,128,128]{2,1,0:T(8,128)S(1)}, f32[4,2,64,128]{3,2,1,0:T(8,128)}, f32[4,2,64,128]{3,2,1,0:T(8,128)}, f32[4,2,64,128]{3,2,1,0:...) while((s32[]{:T(128)}, f32[2,128,128]{2,1,0:T(8,128)S(1)}, ...), condition=%wide.region_28.30_spmd.clone.clone, body=%wide.region_17.29_spmd.clone.clone.sunk | while | flops 283874368 | bytes 5495781 | solution.py:141
  605.1 9.8 %custom-call.43 = f32[2,1,64,64]{2,3,1,0:T(8,128)S(1)} custom-call(f32[2,1,64,64]{3,2,1,0:T(8,128)S(1)} %add_bitcast_fusion.3), custom_call_target="InvertDiagBlocksLowerTriangular" | custom-call | tf_op jit(solution)/shard_map/transpose(jvp())/while/body/eval_jaxpr/triangular_solve | solution.py:110
  624.6 1.7 fusion.374
  629.6 1.7 fusion.364
  637.0 9.8 %custom-call.43 = f32[2,1,64,64]{2,3,1,0:T(8,128)S(1)} custom-call(f32[2,1,64,64]{3,2,1,0:T(8,128)S(1)} %add_bitcast_fusion.3), custom_call_target="InvertDiagBlocksLowerTriangular" | custom-call | tf_op jit(solution)/shard_map/transpose(jvp())/while/body/eval_jaxpr/triangular_solve | solution.py:110
  656.5 1.7 fusion.374
  661.6 1.7 fusion.364
  668.9 9.8 %custom-call.43 = f32[2,1,64,64]{2,3,1,0:T(8,128)S(1)} custom-call(f32[2,1,64,64]{3,2,1,0:T(8,128)S(1)} %add_bitcast_fusion.3), custom_call_target="InvertDiagBlocksLowerTriangular" | custom-call | tf_op jit(solution)/shard_map/transpose(jvp())/while/body/eval_jaxpr/triangular_solve | solution.py:110
  688.4 1.7 fusion.374
  693.4 1.7 fusion.364
  700.8 9.8 %custom-call.43 = f32[2,1,64,64]{2,3,1,0:T(8,128)S(1)} custom-call(f32[2,1,64,64]{3,2,1,0:T(8,128)S(1)} %add_bitcast_fusion.3), custom_call_target="InvertDiagBlocksLowerTriangular" | custom-call | tf_op jit(solution)/shard_map/transpose(jvp())/while/body/eval_jaxpr/triangular_solve | solution.py:110
  720.3 1.7 fusion.374
  725.3 1.7 fusion.364
  732.1 1.5 multiply_reduce_fusion.3
  733.9 4.1 collective-permute-start.1
  739.8 55.8 %all-reduce.15 = (f32[4,512]{1,0:T(4,128)}, f32[128]{0:T(128)S(1)}) all-reduce(f32[4,512]{1,0:T(4,128)S(1)} %pad_add_fusion.5, f32[128]{0:T(128)S(1)} %copy-done.20), channel_id=1, replica_groups=mesh['dp'=8,'ctx'=32] {'ctx'}, use_global_device_ids=true, to_apply=%region_37.39 | all-reduce | flops 2176 | bytes 17408 | tf_op jit(solution)/shard_map/psum | solution.py:240
  795.5 23.8 %psum.23 = f32[128]{0:T(128)} all-reduce(f32[128]{0:T(128)S(1)} %get-tuple-element.2523), channel_id=1, replica_groups=mesh['dp'=8,'ctx'=32] {'dp'}, use_global_device_ids=true, to_apply=%region_40.42 | all-reduce | flops 128 | bytes 1024 | tf_op jit(solution)/shard_map/psum | solution.py:241
  (632 shorter events, 255.0 us)
Async XLA Ops:
  7.2 353.8 %copy-start = (bf16[256,1024]{1,0:T(8,128)(2,1)S(1)}, bf16[256,1024]{1,0:T(8,128)(2,1)}, u32[]{:S(2)}) copy-start(bf16[256,1024]{1,0:T(8,128)(2,1)} %param.28) | copy-start | bytes 1572868
  7.2 133.0 %all-gather.9.cloned.1.call-start = ((), (), s32[]{:S(2)}) async-start(), calls=%async_computation.5 | async-start | bytes 4325376 | tf_op jit(solution)/shard_map/all_gather | solution.py:30
  8.0 8.4 %collective-permute-start = (bf16[3,512]{1,0:T(4,128)(2,1)S(1)}, bf16[3,512]{1,0:T(4,128)(2,1)S(1)}, u32[]{:S(2)}, u32[]{:S(2)}) collective-permute-start(bf16[3,512]{1,0:T(4,128)(2,1)S(1)} %slice.122), channel_id=1, source_target_pairs={{0,1},{1,2},{2,3},{3,4},{4,5},{5,6},{6,7},{7,8},{8,9},{9,10},{10,1... | collective-permute-start | bytes 9224 | tf_op jit(solution)/shard_map/ppermute | solution.py:25
  10.8 8.4 %copy-start.9 = (f32[1,512]{1,0:T(1,128)}, f32[1,512]{1,0:T(1,128)S(1)}, u32[]{:S(2)}) copy-start(f32[1,512]{1,0:T(1,128)S(1)} %get-tuple-element.2583) | copy-start | bytes 6148
  10.8 8.4 %copy-start.11 = (f32[1,512]{1,0:T(1,128)}, f32[1,512]{1,0:T(1,128)S(1)}, u32[]{:S(2)}) copy-start(f32[1,512]{1,0:T(1,128)S(1)} %get-tuple-element.2584) | copy-start | bytes 6148
  18.6 0.9 copy-start.3
  18.7 0.7 copy-start.16
  18.7 0.7 copy-start.17
  18.8 0.6 copy-start.15
  19.2 54.2 %copy-start.8 = (bf16[32,1024]{1,0:T(8,128)(2,1)S(1)}, bf16[32,1024]{1,0:T(8,128)(2,1)}, u32[]{:S(2)}) copy-start(bf16[32,1024]{1,0:T(8,128)(2,1)} %param.29) | copy-start | bytes 196612
  71.7 9.0 %copy-start.2 = (f32[2,128,128]{1,2,0:T(8,128)}, f32[2,128,128]{1,2,0:T(8,128)S(1)}, u32[]{:S(2)}) copy-start(f32[2,128,128]{1,2,0:T(8,128)S(1)} %get-tuple-element.1689) | copy-start | bytes 393220
  72.5 135.3 %all-gather.11.cloned.1.call-start = ((), (), s32[]{:S(2)}) async-start(), calls=%async_computation.6 | async-start | bytes 4325376 | tf_op jit(solution)/shard_map/all_gather | solution.py:30
  74.2 286.8 %all-to-all-start = ((bf16[8,32,1024]{2,1,0:T(8,128)(2,1)}), bf16[8,32,1024]{2,1,0:T(8,128)(2,1)}, u32[]{:S(2)}, u32[]{:S(2)}) async-start(bf16[8,32,1024]{2,1,0:T(8,128)(2,1)} %stack.2), calls=%async_computation.1 | async-start | bytes 1048576 | tf_op jit(solution)/shard_map/all_to_all | solution.py:18
  80.5 305.2 %all-gather.13.cloned.1.call-start = ((), (), s32[]{:S(2)}) async-start(), calls=%async_computation.7 | async-start | bytes 4325376 | tf_op jit(solution)/shard_map/all_gather | solution.py:30
  81.3 399.6 %reduce-scatter.5.cloned.1.call-start = ((), (), s32[]{:S(2)}) async-start(), calls=%async_computation.4 | async-start | bytes 540672 | tf_op jit(solution)/shard_map/reduce_scatter | solution.py:220
  284.5 76.5 %copy-start.19 = (f32[128]{0:T(128)S(1)}, f32[128]{0:T(128)}, u32[]{:S(2)}) copy-start(f32[128]{0:T(128)} %param.27) | copy-start | bytes 1540
  360.7 5.1 copy-start.5
  360.7 5.1 copy-start.6
  365.8 179.8 %all-gather.15.cloned.1.call-start = ((), (), s32[]{:S(2)}) async-start(), calls=%async_computation.8 | async-start | bytes 4325376 | tf_op jit(solution)/shard_map/all_gather | solution.py:30
  384.5 0.7 copy-start.1
  385.2 434.4 %reduce-scatter.3.cloned.1.call-start = ((), (), s32[]{:S(2)}) async-start(), calls=%async_computation.3 | async-start | bytes 589824 | tf_op jit(solution)/shard_map/reduce_scatter | solution.py:212
  599.3 131.0 %copy-start.4 = (f32[256,1,512]{2,0,1:T(8,128)S(1)}, f32[256,1,512]{2,0,1:T(8,128)}, u32[]{:S(2)}) copy-start(f32[256,1,512]{2,0,1:T(8,128)} %copy-done.3) | copy-start | bytes 1572868
  727.0 6.6 copy-start.10
  727.0 6.6 copy-start.12
  733.5 4.8 copy-start.14
  733.5 4.9 copy-start.13
  733.6 5.6 copy-start.18
  733.6 6.2 copy-start.20
  733.9 85.5 %collective-permute-start.1 = (f32[3,512]{1,0:T(4,128)S(1)}, f32[3,512]{1,0:T(4,128)S(1)}, u32[]{:S(2)}, u32[]{:S(2)}) collective-permute-start(f32[3,512]{1,0:T(4,128)S(1)} %pad_add_fusion.4), channel_id=1, source_target_pairs={{1,0},{2,1},{3,2},{4,3},{5,4},{6,5},{7,6},{8,7},{9,8},{10,9},{11,1... | collective-permute-start | bytes 18440 | tf_op jit(solution)/shard_map/ppermute | solution.py:25
  819.5 0.7 copy-start.7
Sparse Core Ops, SparseCore 0:
  72.6 67.4 all-gather.8
  142.0 65.7 all-gather.10
  209.7 66.4 all-gather.12
  365.9 114.9 reduce-scatter.4
  482.7 62.8 all-gather.14
  550.4 75.5 reduce-scatter.2
